TPU v7x, 32 devices: a whole 2x2x4 slice. The times are simulated.
32 devices in a mesh: space: 4 (over y, x), orb: 8 (over z, core).
Axes of the slice: x: 2, y: 2, z: 4, core: 2. Of those that a mesh axis runs over, the one named last changes fastest.
Arguments:
- orbitals: float32 [16, 16, 32, 1024], P('space', None, None, 'orb'), may hold values from -6 to 6
- potential: float32 [16, 16, 32], P('space'), may hold values from 0 to 2
Outputs:
- updated: float32 [16, 16, 32, 1024], P('space', None, None, 'orb')
All inputs are finite; a program needn't handle non-finite values.
Results may differ from a plain program's by a relative error of at most 0.00007.
Values sent between devices are 32-bit elements; how exact they have to be, the bound alone decides.
A program may use at most 64 MiB of HBM per device.

v0:
```python
import jax
import jax.numpy as jnp
from jax import lax
from jax.sharding import PartitionSpec as P

PANEL = 512
DEGREE = 4
STENCIL = (-205.0 / 72.0, 8.0 / 5.0, -1.0 / 5.0, 8.0 / 315.0, -1.0 / 560.0)
SHIFT_MID = 7.25
HALF_WIDTH = 4.75


def padded_2(shard, sides, width):
    for axis, dim in sides:
        count, length = (lax.axis_size(axis), shard.shape[dim])
        up = [(i, (i + 1) % count) for i in range(count)]
        down = [(j, i) for i, j in up]
        last = lax.slice_in_dim(shard, length - width, length, axis=dim)
        leading = lax.slice_in_dim(shard, 0, width, axis=dim)
        before = lax.ppermute(last, axis, up)
        after = lax.ppermute(leading, axis, down)
        shard = jnp.concatenate([before, shard, after], axis=dim)
    return shard


def hamilton(field, potential):
    planes = field.shape[0]
    padded = padded_2(field, (("space", 0),), 4)
    laplace = 3.0 * STENCIL[0] * field
    for offset in range(1, 5):
        upper = padded[4 + offset : 4 + offset + planes]
        below = padded[4 - offset : 4 - offset + planes]
        laplace = laplace + STENCIL[offset] * (upper + below)
    for axis in (1, 2):
        for offset in range(1, 5):
            laplace = laplace + STENCIL[offset] * (
                jnp.roll(field, offset, axis) + jnp.roll(field, -offset, axis)
            )
    return -0.5 * laplace + potential[..., None] * field


def chebyshev(block, potential):
    before = block
    current = (hamilton(block, potential) - SHIFT_MID * block) / HALF_WIDTH
    for order in range(DEGREE - 1):
        following = 2.0 * (hamilton(current, potential) - SHIFT_MID * current) / HALF_WIDTH - before
        before, current = (current, following)
    return current


def per_device(orbitals, potential):
    highest = lax.Precision.HIGHEST
    filtered = chebyshev(orbitals, potential)
    planes, rows_y, rows_z, columns = filtered.shape
    local_points = planes * rows_y * rows_z
    points = local_points * lax.axis_size("space")
    panel_dev = PANEL // lax.axis_size("orb")
    flat = filtered.reshape(local_points, columns)
    panel_own = flat[:, :panel_dev]
    trailing = flat[:, panel_dev:]
    panel = lax.all_gather(panel_own, "orb", axis=1, tiled=True)
    coupling_part = jnp.dot(panel.T, trailing, precision=highest)
    gram_part = jnp.dot(panel.T, panel, precision=highest)
    gram_full, coupling = lax.psum((gram_part, coupling_part), "space")
    gram_full = gram_full / points
    coupling = coupling / points
    lower_factor = jnp.linalg.cholesky(gram_full)
    identity = jnp.eye(PANEL, dtype=jnp.float32)
    inverse = lax.linalg.triangular_solve(lower_factor, identity, left_side=True, lower=True)
    start = lax.axis_index("orb") * panel_dev
    own_rows = lax.dynamic_slice_in_dim(inverse, start, panel_dev, 0)
    ortho_own = jnp.dot(panel, own_rows.T, precision=highest)
    middle = jnp.dot(inverse, coupling, precision=highest)
    project = jnp.dot(inverse.T, middle, precision=highest)
    trailing_new = trailing - jnp.dot(panel, project, precision=highest)
    joined = jnp.concatenate([ortho_own, trailing_new], axis=1)
    return joined.reshape(planes, rows_y, rows_z, columns)


def solution(mesh):
    placed = (P("space", None, None, "orb"), P("space", None, None))
    return jax.shard_map(
        per_device,
        mesh=mesh,
        in_specs=placed,
        out_specs=P("space", None, None, "orb"),
        check_vma=False,
    )
```

profile of v0, /device:TPU:0, one launch (start us, length us, event | category | flops | bytes accessed | tf_op | source)
XLA Modules:
  0.0 514.7 jit_solution(1693416008679827727)
XLA Ops:
  21.2 13.6 %collective-permute-done.1 = f32[4,16,32,128]{3,2,1,0:T(8,128)S(1)} collective-permute-done((f32[4,16,32,128]{3,2,1,0:T(8,128)}, f32[4,16,32,128]{3,2,1,0:T(8,128)S(1)}, u32[]{:S(2)}, u32[]{:S(2)}) %collective-permute-start.1) | collective-permute-done | bytes 1048608 | tf_op jit(solution)/shard_map/ppermute | solution.py:20
  35.0 21.6 %collective-permute-done = f32[4,16,32,128]{3,2,1,0:T(8,128)S(1)} collective-permute-done((f32[4,16,32,128]{3,2,1,0:T(8,128)}, f32[4,16,32,128]{3,2,1,0:T(8,128)S(1)}, u32[]{:S(2)}, u32[]{:S(2)}) %collective-permute-start) | collective-permute-done | bytes 1048608 | tf_op jit(solution)/shard_map/ppermute | solution.py:21
  56.6 5.3 %broadcast_multiply_fusion.1 = (f32[4,16,32,128]{3,2,1,0:T(8,128)S(1)}, f32[4,16,32,128]{3,2,1,0:T(8,128)S(1)}) fusion(f32[4,16,32,128]{3,2,1,0:T(8,128)S(1)} %copy-done, f32[4,16,32]{2,1,0:T(8,128)S(1)} %copy-done.12, f32[4,16,4,128]{3,2,1,0:T(4,128)} %get-tuple-element.156, f32[4,16,28,128]{3,2,1,0:T(8,128)S(1)} %get-tuple-element.158, ...), kind=kLoop, calls=%fused_computation.211 | loop fusion | flops 15466496 | bytes 28319744 | tf_op jit(solution)/shard_map/div | solution.py:44
  72.9 22.7 %collective-permute-done.2 = f32[4,16,32,128]{3,2,1,0:T(8,128)S(1)} collective-permute-done((f32[4,16,32,128]{3,2,1,0:T(8,128)S(1)}, f32[4,16,32,128]{3,2,1,0:T(8,128)S(1)}, u32[]{:S(2)}, u32[]{:S(2)}) %collective-permute-start.2) | collective-permute-done | bytes 1048608 | tf_op jit(solution)/shard_map/ppermute | solution.py:21
  95.6 20.6 %collective-permute-done.3 = f32[4,16,32,128]{3,2,1,0:T(8,128)S(1)} collective-permute-done((f32[4,16,32,128]{3,2,1,0:T(8,128)S(1)}, f32[4,16,32,128]{3,2,1,0:T(8,128)S(1)}, u32[]{:S(2)}, u32[]{:S(2)}) %collective-permute-start.3) | collective-permute-done | bytes 1048608 | tf_op jit(solution)/shard_map/ppermute | solution.py:20
  117.2 6.9 %multiply_subtract_fusion.2 = f32[4,16,32,128]{3,2,1,0:T(8,128)S(1)} fusion(f32[4,16,32,128]{3,2,1,0:T(8,128)S(1)} %copy-done, f32[4,16,32,128]{3,2,1,0:T(8,128)S(1)} %get-tuple-element.24, f32[4,16,4,128]{3,2,1,0:T(4,128)} %get-tuple-element.122, f32[4,16,28,128]{3,2,1,0:T(8,128)S(1)} %get-tuple-element.124, f32[4,16,28,128]{3,2,1,0:T(8,128)S(1)} %get-tuple-element.123, ...), kind=kLoop, calls=%fused_computation.201 | loop fusion | flops 17301504 | bytes 23076864 | tf_op jit(solution)/shard_map/sub | solution.py:46
  135.1 17.0 %collective-permute-done.4 = f32[4,16,32,128]{3,2,1,0:T(8,128)S(1)} collective-permute-done((f32[4,16,32,128]{3,2,1,0:T(8,128)S(1)}, f32[4,16,32,128]{3,2,1,0:T(8,128)S(1)}, u32[]{:S(2)}, u32[]{:S(2)}) %collective-permute-start.4) | collective-permute-done | bytes 1048608 | tf_op jit(solution)/shard_map/ppermute | solution.py:21
  152.1 20.4 %collective-permute-done.5 = f32[4,16,32,128]{3,2,1,0:T(8,128)S(1)} collective-permute-done((f32[4,16,32,128]{3,2,1,0:T(8,128)S(1)}, f32[4,16,32,128]{3,2,1,0:T(8,128)S(1)}, u32[]{:S(2)}, u32[]{:S(2)}) %collective-permute-start.5) | collective-permute-done | bytes 1048608 | tf_op jit(solution)/shard_map/ppermute | solution.py:20
  173.5 6.9 %multiply_subtract_fusion.1 = f32[4,16,32,128]{3,2,1,0:T(8,128)S(1)} fusion(f32[4,16,32,128]{3,2,1,0:T(8,128)S(1)} %multiply_subtract_fusion.2, f32[4,16,4,128]{3,2,1,0:T(4,128)} %get-tuple-element.90, f32[4,16,28,128]{3,2,1,0:T(8,128)S(1)} %get-tuple-element.92, f32[4,16,28,128]{3,2,1,0:T(8,128)S(1)} %get-tuple-element.91, ...), kind=kLoop, calls=%fused_computation.200 | loop fusion | flops 17563648 | bytes 22028288 | tf_op jit(solution)/shard_map/sub | solution.py:46
  190.4 18.2 %collective-permute-done.6 = f32[4,16,32,128]{3,2,1,0:T(8,128)S(1)} collective-permute-done((f32[4,16,32,128]{3,2,1,0:T(8,128)S(1)}, f32[4,16,32,128]{3,2,1,0:T(8,128)S(1)}, u32[]{:S(2)}, u32[]{:S(2)}) %collective-permute-start.6) | collective-permute-done | bytes 1048608 | tf_op jit(solution)/shard_map/ppermute | solution.py:21
  208.7 19.4 %collective-permute-done.7 = f32[4,16,32,128]{3,2,1,0:T(8,128)S(1)} collective-permute-done((f32[4,16,32,128]{3,2,1,0:T(8,128)S(1)}, f32[4,16,32,128]{3,2,1,0:T(8,128)S(1)}, u32[]{:S(2)}, u32[]{:S(2)}) %collective-permute-start.7) | collective-permute-done | bytes 1048608 | tf_op jit(solution)/shard_map/ppermute | solution.py:20
  229.1 6.8 %multiply_subtract_fusion = f32[4,16,32,128]{3,2,1,0:T(8,128)S(1)} fusion(f32[4,16,32,128]{3,2,1,0:T(8,128)S(1)} %multiply_subtract_fusion.2, f32[4,16,32,128]{3,2,1,0:T(8,128)S(1)} %multiply_subtract_fusion.1, f32[4,16,4,128]{3,2,1,0:T(4,128)} %get-tuple-element.58, f32[4,16,28,128]{3,2,1,0:T(8,128)S(1)} %get-tuple-element.60, ...), kind=kLoop, calls=%fused_computation.199 | loop fusion | flops 17301504 | bytes 22028288 | tf_op jit(solution)/shard_map/sub | solution.py:46
  237.5 47.5 %all-gather.2.cloned.1.call-done = f32[2048,512]{0,1:T(8,128)} async-done(((f32[2048,64]{0,1:T(8,128)}), f32[2048,512]{0,1:T(8,128)}) %all-gather.2.cloned.1.call-update) | async-done | bytes 4194320 | tf_op jit(solution)/shard_map/all_gather | solution.py:61
  285.0 10.7 %fusion.224 = f32[512,512]{0,1:T(8,128)} fusion(f32[2048,512]{0,1:T(8,128)} %all-gather.2.cloned.1.call-done), kind=kOutput, calls=%fused_computation.337 | convolution fusion | flops 6442450944 | bytes 5242880 | tf_op jit(solution)/shard_map/dot_general | solution.py:63
  303.0 51.0 %all-reduce.4.cloned.1.call-done = (f32[512,64]{0,1:T(8,128)}, f32[512,512]{0,1:T(8,128)}) async-done(((f32[512,64]{0,1:T(8,128)}, f32[512,512]{0,1:T(8,128)}), (f32[512,64]{0,1:T(8,128)}, f32[512,512]{0,1:T(8,128)})) %all-reduce.4.cloned.1.call-update) | async-done | bytes 1179664 | tf_op jit(solution)/shard_map/psum | solution.py:64
  356.0 11.7 %cholesky.104 = f32[128,128]{1,0:T(8,128)S(1)} custom-call(f32[128,128]{1,0:T(8,128)S(1)} %cholesky.266), custom_call_target="Cholesky" | custom-call | tf_op jit(solution)/shard_map/jit(cholesky)/cholesky | solution.py:67
  367.9 9.8 %custom-call.30 = f32[1,128,128]{1,2,0:T(8,128)S(1)} custom-call(f32[1,128,128]{2,1,0:T(8,128)S(1)} %get-tuple-element.168), custom_call_target="InvertDiagBlocksLowerTriangular" | custom-call | tf_op jit(solution)/shard_map/jit(cholesky)/cholesky | solution.py:67
  378.4 11.9 %cholesky.217 = f32[128,128]{1,0:T(8,128)S(1)} custom-call(f32[128,128]{1,0:T(8,128)S(1)} %cholesky.270), custom_call_target="Cholesky" | custom-call | tf_op jit(solution)/shard_map/jit(cholesky)/cholesky | solution.py:67
  390.3 9.8 %custom-call.31 = f32[1,128,128]{1,2,0:T(8,128)S(1)} custom-call(f32[1,128,128]{2,1,0:T(8,128)S(1)} %get-tuple-element.165), custom_call_target="InvertDiagBlocksLowerTriangular" | custom-call | tf_op jit(solution)/shard_map/jit(cholesky)/cholesky | solution.py:67
  400.8 12.3 %cholesky.238 = f32[128,128]{1,0:T(8,128)} custom-call(f32[128,128]{1,0:T(8,128)S(1)} %cholesky.275), custom_call_target="Cholesky" | custom-call | tf_op jit(solution)/shard_map/jit(cholesky)/cholesky | solution.py:67
  415.4 11.3 %custom-call.32 = f32[1,128,128]{1,2,0:T(8,128)} custom-call(f32[1,128,128]{2,1,0:T(8,128)} %get-tuple-element.162), custom_call_target="InvertDiagBlocksLowerTriangular" | custom-call | tf_op jit(solution)/shard_map/jit(cholesky)/cholesky | solution.py:67
  428.1 11.9 %cholesky.255 = f32[128,128]{1,0:T(8,128)S(1)} custom-call(f32[128,128]{1,0:T(8,128)S(1)} %convolution_subtract_fusion.6), custom_call_target="Cholesky" | custom-call | tf_op jit(solution)/shard_map/jit(cholesky)/cholesky | solution.py:67
  444.2 10.8 %while.1 = (s32[]{:T(128)}, f32[512,512]{1,0:T(8,128)S(1)}, s32[4,2]{0,1:T(2,128)S(1)}, f32[4,128,128]{2,1,0:T(8,128)}, s32[]{:T(128)}) while((s32[]{:T(128)}, f32[512,512]{1,0:T(8,128)S(1)}, s32[4,2]{0,1:T(2,128)S(1)}, f32[4,128,128]{2,1,0:T(8,128)}, s32[]{:T(128)}) %tuple.94), condition=%wide.while_cond, body=%wide.while_body.sunk | while | flops 2 | bytes 132705 | solution.py:69
  455.0 40.1 %custom-call.33 = f32[4,128,128]{1,2,0:T(8,128)S(1)} custom-call(f32[4,128,128]{2,1,0:T(8,128)} %get-tuple-element.12), custom_call_target="InvertDiagBlocksLowerTriangular" | custom-call | tf_op jit(solution)/shard_map/triangular_solve | solution.py:69
  (166 shorter events, 90.2 us)
Async XLA Ops:
  6.5 5.8 %copy-start = (f32[4,16,32,128]{3,2,1,0:T(8,128)S(1)}, f32[4,16,32,128]{3,2,1,0:T(8,128)}, u32[]{:S(2)}) copy-start(f32[4,16,32,128]{3,2,1,0:T(8,128)} %param.2) | copy-start | bytes 3145732
  6.5 278.4 %all-gather.2.cloned.1.call-start = ((), (), s32[]{:S(2)}) async-start(), calls=%async_computation | async-start | bytes 4718592 | tf_op jit(solution)/shard_map/all_gather | solution.py:61
  6.5 28.2 %collective-permute-start.1 = (f32[4,16,32,128]{3,2,1,0:T(8,128)}, f32[4,16,32,128]{3,2,1,0:T(8,128)S(1)}, u32[]{:S(2)}, u32[]{:S(2)}) collective-permute-start(f32[4,16,32,128]{3,2,1,0:T(8,128)} %param.2), channel_id=1, source_target_pairs={{0,8},{8,16},{16,24},{24,0},{1,9},{9,17},{17,25},{25,1},{2,10},{10... | collective-permute-start | bytes 3145736 | tf_op jit(solution)/shard_map/ppermute | solution.py:20
  9.5 47.0 %collective-permute-start = (f32[4,16,32,128]{3,2,1,0:T(8,128)}, f32[4,16,32,128]{3,2,1,0:T(8,128)S(1)}, u32[]{:S(2)}, u32[]{:S(2)}) collective-permute-start(f32[4,16,32,128]{3,2,1,0:T(8,128)} %param.2), channel_id=1, source_target_pairs={{8,0},{16,8},{24,16},{0,24},{9,1},{17,9},{25,17},{1,25},{10,2},{18... | collective-permute-start | bytes 3145736 | tf_op jit(solution)/shard_map/ppermute | solution.py:21
  16.4 4.3 copy-start.12
  69.5 26.0 %collective-permute-start.2 = (f32[4,16,32,128]{3,2,1,0:T(8,128)S(1)}, f32[4,16,32,128]{3,2,1,0:T(8,128)S(1)}, u32[]{:S(2)}, u32[]{:S(2)}) collective-permute-start(f32[4,16,32,128]{3,2,1,0:T(8,128)S(1)} %get-tuple-element.23), channel_id=1, source_target_pairs={{8,0},{16,8},{24,16},{0,24},{9,1},{17,9},{25,17},{1,25},{10,2},{18... | collective-permute-start | bytes 3145736 | tf_op jit(solution)/shard_map/ppermute | solution.py:21
  71.0 45.2 %collective-permute-start.3 = (f32[4,16,32,128]{3,2,1,0:T(8,128)S(1)}, f32[4,16,32,128]{3,2,1,0:T(8,128)S(1)}, u32[]{:S(2)}, u32[]{:S(2)}) collective-permute-start(f32[4,16,32,128]{3,2,1,0:T(8,128)S(1)} %get-tuple-element.23), channel_id=1, source_target_pairs={{0,8},{8,16},{16,24},{24,0},{1,9},{9,17},{17,25},{25,1},{2,10},{10... | collective-permute-start | bytes 3145736 | tf_op jit(solution)/shard_map/ppermute | solution.py:20
  95.6 20.6 %copy-start.10 = (f32[4,16,32,128]{3,2,1,0:T(8,128)}, f32[4,16,32,128]{3,2,1,0:T(8,128)S(1)}, u32[]{:S(2)}) copy-start(f32[4,16,32,128]{3,2,1,0:T(8,128)S(1)} %collective-permute-done.2) | copy-start | bytes 3145732
  116.2 1.0 copy-start.11
  126.0 26.0 %collective-permute-start.4 = (f32[4,16,32,128]{3,2,1,0:T(8,128)S(1)}, f32[4,16,32,128]{3,2,1,0:T(8,128)S(1)}, u32[]{:S(2)}, u32[]{:S(2)}) collective-permute-start(f32[4,16,32,128]{3,2,1,0:T(8,128)S(1)} %multiply_subtract_fusion.2), channel_id=1, source_target_pairs={{8,0},{16,8},{24,16},{0,24},{9,1},{17,9},{25,17},{1,25},{10,2},{18... | collective-permute-start | bytes 3145736 | tf_op jit(solution)/shard_map/ppermute | solution.py:21
  128.3 44.2 %collective-permute-start.5 = (f32[4,16,32,128]{3,2,1,0:T(8,128)S(1)}, f32[4,16,32,128]{3,2,1,0:T(8,128)S(1)}, u32[]{:S(2)}, u32[]{:S(2)}) collective-permute-start(f32[4,16,32,128]{3,2,1,0:T(8,128)S(1)} %multiply_subtract_fusion.2), channel_id=1, source_target_pairs={{0,8},{8,16},{16,24},{24,0},{1,9},{9,17},{17,25},{25,1},{2,10},{10... | collective-permute-start | bytes 3145736 | tf_op jit(solution)/shard_map/ppermute | solution.py:20
  152.1 20.4 %copy-start.7 = (f32[4,16,32,128]{3,2,1,0:T(8,128)}, f32[4,16,32,128]{3,2,1,0:T(8,128)S(1)}, u32[]{:S(2)}) copy-start(f32[4,16,32,128]{3,2,1,0:T(8,128)S(1)} %collective-permute-done.4) | copy-start | bytes 3145732
  172.5 1.0 copy-start.9
  182.6 26.0 %collective-permute-start.6 = (f32[4,16,32,128]{3,2,1,0:T(8,128)S(1)}, f32[4,16,32,128]{3,2,1,0:T(8,128)S(1)}, u32[]{:S(2)}, u32[]{:S(2)}) collective-permute-start(f32[4,16,32,128]{3,2,1,0:T(8,128)S(1)} %multiply_subtract_fusion.1), channel_id=1, source_target_pairs={{8,0},{16,8},{24,16},{0,24},{9,1},{17,9},{25,17},{1,25},{10,2},{18... | collective-permute-start | bytes 3145736 | tf_op jit(solution)/shard_map/ppermute | solution.py:21
  184.1 44.0 %collective-permute-start.7 = (f32[4,16,32,128]{3,2,1,0:T(8,128)S(1)}, f32[4,16,32,128]{3,2,1,0:T(8,128)S(1)}, u32[]{:S(2)}, u32[]{:S(2)}) collective-permute-start(f32[4,16,32,128]{3,2,1,0:T(8,128)S(1)} %multiply_subtract_fusion.1), channel_id=1, source_target_pairs={{0,8},{8,16},{16,24},{24,0},{1,9},{9,17},{17,25},{25,1},{2,10},{10... | collective-permute-start | bytes 3145736 | tf_op jit(solution)/shard_map/ppermute | solution.py:20
  190.2 38.9 %copy-start.13 = (f32[4,16,32]{2,1,0:T(8,128)S(1)}, f32[4,16,32]{2,1,0:T(8,128)}, u32[]{:S(2)}) copy-start(f32[4,16,32]{2,1,0:T(8,128)} %param.3) | copy-start | bytes 24580
  208.7 19.4 %copy-start.6 = (f32[4,16,32,128]{3,2,1,0:T(8,128)}, f32[4,16,32,128]{3,2,1,0:T(8,128)S(1)}, u32[]{:S(2)}) copy-start(f32[4,16,32,128]{3,2,1,0:T(8,128)S(1)} %collective-permute-done.6) | copy-start | bytes 3145732
  237.4 116.6 %all-reduce.4.cloned.1.call-start = ((), (), s32[]{:S(2)}) async-start(), calls=%async_computation.1 | async-start | bytes 2359296 | tf_op jit(solution)/shard_map/psum | solution.py:64
  285.0 10.7 %copy-start.1 = (f32[2048,512]{0,1:T(8,128)S(1)}, f32[2048,512]{0,1:T(8,128)}, u32[]{:S(2)}) copy-start(f32[2048,512]{0,1:T(8,128)} %all-gather.2.cloned.1.call-done) | copy-start | bytes 12582916
  354.0 1.8 copy-start.3
  413.1 82.3 %copy-start.4 = (f32[512,512]{1,0:T(8,128)S(1)}, f32[512,512]{1,0:T(8,128)}, u32[]{:S(2)}) copy-start(f32[512,512]{1,0:T(8,128)} %fusion.125) | copy-start | bytes 3145732
  497.1 1.2 copy-start.14
  498.2 2.2 copy-start.2
  500.4 2.9 copy-start.5
  (1 other events, 1.0 us)
Sparse Core Ops, SparseCore 0:
  237.5 47.3 all-gather.1
  300.8 53.1 all-reduce.3
where the time goes:
time: 522 us; the launch traced here: 515 us
  waiting for transfers between devices  252 us (48%)
  other arithmetic  152 us (29%)
  local copies, waits for them, and re-layouts  54.5 us (10%)
  matrix products  29 us (6%)
  between operations  17 us (3%)
  starting transfers between devices  10.5 us (2%)
    another operation x14, other arithmetic, per_device(): lower_factor = jnp.linalg.cholesky(gram_full)  82.5 us
    ppermute x4, waiting for transfers between devices, padded_2(): after = lax.ppermute(leading, axis, down)  79.4 us
    ppermute x4, waiting for transfers between devices, padded_2(): before = lax.ppermute(last, axis, up)  74 us
    psum x1, waiting for transfers between devices, per_device(): gram_full, coupling = lax.psum((gram_part, coupling_part), 'space')  51 us
    all_gather x1, waiting for transfers between devices, per_device(): panel = lax.all_gather(panel_own, 'orb', axis=1, tiled=True)  47.5 us
    another operation x4, other arithmetic, per_device(): lax.linalg.triangular_solve(lower_factor, identity, left_side=True, lower...  40.3 us
    slice x64, local copies, waits for them, and re-layouts, hamilton(): jnp.roll(field, offset, axis) + jnp.roll(field, -offset, axis)  35.9 us
    sub x3, other arithmetic, chebyshev(): 2.0 * (hamilton(current, potential) - SHIFT_MID * current) / HALF_WIDTH  20.7 us
  transfers between devices with their start and end apart: 10, of which 10 were waited for; matrix products, arithmetic and copies ran while one was open for 5% of the time, Pallas kernels for 0%

commit v1 on v0

--- a/solution.py
+++ b/solution.py
@@ -58,7 +58,14 @@
     flat = filtered.reshape(local_points, columns)
     panel_own = flat[:, :panel_dev]
     trailing = flat[:, panel_dev:]
-    panel = lax.all_gather(panel_own, "orb", axis=1, tiled=True)
+    ways, here, turn = (lax.axis_size("orb"), lax.axis_index("orb"), panel_own.shape[1])
+    line, have = (panel_own, 1)
+    while have < ways:
+        line = jnp.concatenate(
+            [line, lax.ppermute(line, "orb", [(d, (d - have) % ways) for d in range(ways)])], axis=1
+        )
+        have = 2 * have
+    panel = jnp.roll(line, here * turn, axis=1)
     coupling_part = jnp.dot(panel.T, trailing, precision=highest)
     gram_part = jnp.dot(panel.T, panel, precision=highest)
     gram_full, coupling = lax.psum((gram_part, coupling_part), "space")

time: 522 us -> 626 us (1.20)
  waiting for transfers between devices: 252 us -> 329 us
  local copies, waits for them, and re-layouts: 54.5 us -> 65.3 us
  matrix products: 29 us -> 38.8 us
    ppermute x0 -> x3, waiting for transfers between devices: none -> 123 us  [per_device(): lax.ppermute(line, 'orb', [(d, (d - have) % ways) for d in range(ways)])]
    all_gather x1 -> x0, waiting for transfers between devices: 47.5 us -> none  [per_device(): panel = lax.all_gather(panel_own, 'orb', axis=1, tiled=True)]
    concatenate x0 -> x1, local copies, waits for them, and re-layouts: none -> 9.97 us  [per_device(): panel = jnp.roll(line, here * turn, axis=1)]
  transfers between devices with their start and end apart: 10 -> 12, of which waited for: 10 -> 12; matrix products, arithmetic and copies ran while one was open for 5% -> 4% of each run, Pallas kernels for 0% -> 0%
where the time goes in v1:
time: 626 us; the launch traced here: 618 us
  waiting for transfers between devices  329 us (53%)
  other arithmetic  154 us (25%)
  local copies, waits for them, and re-layouts  65.3 us (10%)
  matrix products  38.8 us (6%)
  between operations  17 us (3%)
  starting transfers between devices  14.3 us (2%)
    ppermute x3, waiting for transfers between devices, per_device(): lax.ppermute(line, 'orb', [(d, (d - have) % ways) for d in range(ways)])  123 us
    another operation x14, other arithmetic, per_device(): lower_factor = jnp.linalg.cholesky(gram_full)  82.4 us
    ppermute x4, waiting for transfers between devices, padded_2(): after = lax.ppermute(leading, axis, down)  79.4 us
    ppermute x4, waiting for transfers between devices, padded_2(): before = lax.ppermute(last, axis, up)  74 us
    psum x1, waiting for transfers between devices, per_device(): gram_full, coupling = lax.psum((gram_part, coupling_part), 'space')  52.4 us
    another operation x4, other arithmetic, per_device(): lax.linalg.triangular_solve(lower_factor, identity, left_side=True, lower...  40.3 us
    slice x64, local copies, waits for them, and re-layouts, hamilton(): jnp.roll(field, offset, axis) + jnp.roll(field, -offset, axis)  35.9 us
    sub x3, other arithmetic, chebyshev(): 2.0 * (hamilton(current, potential) - SHIFT_MID * current) / HALF_WIDTH  20.7 us
  transfers between devices with their start and end apart: 12, of which 12 were waited for; matrix products, arithmetic and copies ran while one was open for 4% of the time, Pallas kernels for 0%

profile of v1, /device:TPU:0, one launch (start us, length us, event | category | flops | bytes accessed | tf_op | source)
XLA Modules:
  0.0 618.4 jit_solution(2240156497711640495)
XLA Ops:
  21.2 13.6 %collective-permute-done.1 = f32[4,16,32,128]{3,2,1,0:T(8,128)S(1)} collective-permute-done((f32[4,16,32,128]{3,2,1,0:T(8,128)}, f32[4,16,32,128]{3,2,1,0:T(8,128)S(1)}, u32[]{:S(2)}, u32[]{:S(2)}) %collective-permute-start.1) | collective-permute-done | bytes 1048608 | tf_op jit(solution)/shard_map/ppermute | solution.py:20
  35.0 21.6 %collective-permute-done = f32[4,16,32,128]{3,2,1,0:T(8,128)S(1)} collective-permute-done((f32[4,16,32,128]{3,2,1,0:T(8,128)}, f32[4,16,32,128]{3,2,1,0:T(8,128)S(1)}, u32[]{:S(2)}, u32[]{:S(2)}) %collective-permute-start) | collective-permute-done | bytes 1048608 | tf_op jit(solution)/shard_map/ppermute | solution.py:21
  72.9 22.7 %collective-permute-done.2 = f32[4,16,32,128]{3,2,1,0:T(8,128)S(1)} collective-permute-done((f32[4,16,32,128]{3,2,1,0:T(8,128)S(1)}, f32[4,16,32,128]{3,2,1,0:T(8,128)S(1)}, u32[]{:S(2)}, u32[]{:S(2)}) %collective-permute-start.2) | collective-permute-done | bytes 1048608 | tf_op jit(solution)/shard_map/ppermute | solution.py:21
  95.6 20.6 %collective-permute-done.3 = f32[4,16,32,128]{3,2,1,0:T(8,128)S(1)} collective-permute-done((f32[4,16,32,128]{3,2,1,0:T(8,128)S(1)}, f32[4,16,32,128]{3,2,1,0:T(8,128)S(1)}, u32[]{:S(2)}, u32[]{:S(2)}) %collective-permute-start.3) | collective-permute-done | bytes 1048608 | tf_op jit(solution)/shard_map/ppermute | solution.py:20
  117.2 6.9 %multiply_subtract_fusion.2 = f32[4,16,32,128]{3,2,1,0:T(8,128)S(1)} fusion(f32[4,16,32,128]{3,2,1,0:T(8,128)S(1)} %copy-done, f32[4,16,32,128]{3,2,1,0:T(8,128)S(1)} %get-tuple-element.24, f32[4,16,4,128]{3,2,1,0:T(4,128)} %get-tuple-element.122, f32[4,16,28,128]{3,2,1,0:T(8,128)S(1)} %get-tuple-element.124, f32[4,16,28,128]{3,2,1,0:T(8,128)S(1)} %get-tuple-element.123, ...), kind=kLoop, calls=%fused_computation.211 | loop fusion | flops 17301504 | bytes 23076864 | tf_op jit(solution)/shard_map/sub | solution.py:46
  135.1 17.0 %collective-permute-done.4 = f32[4,16,32,128]{3,2,1,0:T(8,128)S(1)} collective-permute-done((f32[4,16,32,128]{3,2,1,0:T(8,128)S(1)}, f32[4,16,32,128]{3,2,1,0:T(8,128)S(1)}, u32[]{:S(2)}, u32[]{:S(2)}) %collective-permute-start.4) | collective-permute-done | bytes 1048608 | tf_op jit(solution)/shard_map/ppermute | solution.py:21
  152.1 20.4 %collective-permute-done.5 = f32[4,16,32,128]{3,2,1,0:T(8,128)S(1)} collective-permute-done((f32[4,16,32,128]{3,2,1,0:T(8,128)S(1)}, f32[4,16,32,128]{3,2,1,0:T(8,128)S(1)}, u32[]{:S(2)}, u32[]{:S(2)}) %collective-permute-start.5) | collective-permute-done | bytes 1048608 | tf_op jit(solution)/shard_map/ppermute | solution.py:20
  173.5 7.0 %multiply_subtract_fusion.1 = f32[4,16,32,128]{3,2,1,0:T(8,128)S(1)} fusion(f32[4,16,32,128]{3,2,1,0:T(8,128)S(1)} %multiply_subtract_fusion.2, f32[4,16,4,128]{3,2,1,0:T(4,128)} %get-tuple-element.90, f32[4,16,28,128]{3,2,1,0:T(8,128)S(1)} %get-tuple-element.92, f32[4,16,28,128]{3,2,1,0:T(8,128)S(1)} %get-tuple-element.91, ...), kind=kLoop, calls=%fused_computation.210 | loop fusion | flops 17563648 | bytes 22028288 | tf_op jit(solution)/shard_map/sub | solution.py:46
  190.5 18.3 %collective-permute-done.6 = f32[4,16,32,128]{3,2,1,0:T(8,128)S(1)} collective-permute-done((f32[4,16,32,128]{3,2,1,0:T(8,128)S(1)}, f32[4,16,32,128]{3,2,1,0:T(8,128)S(1)}, u32[]{:S(2)}, u32[]{:S(2)}) %collective-permute-start.6) | collective-permute-done | bytes 1048608 | tf_op jit(solution)/shard_map/ppermute | solution.py:21
  208.7 19.4 %collective-permute-done.7 = f32[4,16,32,128]{3,2,1,0:T(8,128)S(1)} collective-permute-done((f32[4,16,32,128]{3,2,1,0:T(8,128)S(1)}, f32[4,16,32,128]{3,2,1,0:T(8,128)S(1)}, u32[]{:S(2)}, u32[]{:S(2)}) %collective-permute-start.7) | collective-permute-done | bytes 1048608 | tf_op jit(solution)/shard_map/ppermute | solution.py:20
  249.0 23.2 %collective-permute-done.9 = f32[2048,128]{1,0:T(8,128)S(1)} collective-permute-done((f32[2048,128]{1,0:T(8,128)S(1)}, f32[2048,128]{1,0:T(8,128)S(1)}, u32[]{:S(2)}, u32[]{:S(2)}) %collective-permute-start.9) | collective-permute-done | bytes 1048608 | tf_op jit(solution)/shard_map/ppermute | solution.py:65
  275.0 93.3 %collective-permute-done.10 = f32[2048,256]{1,0:T(8,128)} collective-permute-done((f32[2048,256]{1,0:T(8,128)}, f32[2048,256]{1,0:T(8,128)}, u32[]{:S(2)}, u32[]{:S(2)}) %collective-permute-start.10) | collective-permute-done | bytes 2097184 | tf_op jit(solution)/shard_map/ppermute | solution.py:65
  368.3 10.0 %concatenate.351 = f32[2048,1024]{1,0:T(8,128)} concatenate(f32[2048,64]{1,0:T(8,128)S(1)} %get-tuple-element.27, f32[2048,64]{1,0:T(8,128)S(1)} %copy.14, f32[2048,128]{1,0:T(8,128)} %copy-done.1, f32[2048,256]{1,0:T(8,128)} %collective-permute-done.10, f32[2048,64]{1,0:T(8,128)S(1)} %get-tuple-element.27, f32[2048,64]{1,0:T(8,128)S(1)} %copy.14, f32[2048,128]{1,0:T(8,128)} %copy-done.1, ...), dimensions={1} | concatenate | bytes 16777216 | tf_op jit(solution)/shard_map/jit(_roll_dynamic)/concatenate | solution.py:68
  378.3 13.6 %fusion.6 = f32[512,512]{0,1:T(8,128)} fusion(f32[2048,1024]{1,0:T(8,128)} %concatenate.351, s32[]{:T(128)S(6)} %select_n.21), kind=kOutput, calls=%fused_computation.8 | convolution fusion | flops 6442450944 | bytes 5242884 | tf_op jit(solution)/shard_map/dot_general | solution.py:70
  400.6 52.4 %all-reduce.4.cloned.1.call-done = (f32[512,64]{0,1:T(8,128)}, f32[512,512]{0,1:T(8,128)}) async-done(((f32[512,64]{0,1:T(8,128)}, f32[512,512]{0,1:T(8,128)}), (f32[512,64]{0,1:T(8,128)}, f32[512,512]{0,1:T(8,128)})) %all-reduce.4.cloned.1.call-update) | async-done | bytes 1179664 | tf_op jit(solution)/shard_map/psum | solution.py:71
  455.0 11.7 %cholesky.104 = f32[128,128]{1,0:T(8,128)S(1)} custom-call(f32[128,128]{1,0:T(8,128)S(1)} %cholesky.266), custom_call_target="Cholesky" | custom-call | tf_op jit(solution)/shard_map/jit(cholesky)/cholesky | solution.py:74
  466.9 9.8 %custom-call.30 = f32[1,128,128]{1,2,0:T(8,128)S(1)} custom-call(f32[1,128,128]{2,1,0:T(8,128)S(1)} %get-tuple-element.168), custom_call_target="InvertDiagBlocksLowerTriangular" | custom-call | tf_op jit(solution)/shard_map/jit(cholesky)/cholesky | solution.py:74
  477.4 11.9 %cholesky.217 = f32[128,128]{1,0:T(8,128)S(1)} custom-call(f32[128,128]{1,0:T(8,128)S(1)} %cholesky.270), custom_call_target="Cholesky" | custom-call | tf_op jit(solution)/shard_map/jit(cholesky)/cholesky | solution.py:74
  489.3 9.8 %custom-call.31 = f32[1,128,128]{1,2,0:T(8,128)S(1)} custom-call(f32[1,128,128]{2,1,0:T(8,128)S(1)} %get-tuple-element.165), custom_call_target="InvertDiagBlocksLowerTriangular" | custom-call | tf_op jit(solution)/shard_map/jit(cholesky)/cholesky | solution.py:74
  499.8 12.3 %cholesky.238 = f32[128,128]{1,0:T(8,128)} custom-call(f32[128,128]{1,0:T(8,128)S(1)} %cholesky.275), custom_call_target="Cholesky" | custom-call | tf_op jit(solution)/shard_map/jit(cholesky)/cholesky | solution.py:74
  514.3 11.3 %custom-call.32 = f32[1,128,128]{1,2,0:T(8,128)} custom-call(f32[1,128,128]{2,1,0:T(8,128)} %get-tuple-element.162), custom_call_target="InvertDiagBlocksLowerTriangular" | custom-call | tf_op jit(solution)/shard_map/jit(cholesky)/cholesky | solution.py:74
  527.0 11.9 %cholesky.255 = f32[128,128]{1,0:T(8,128)S(1)} custom-call(f32[128,128]{1,0:T(8,128)S(1)} %convolution_subtract_fusion.5), custom_call_target="Cholesky" | custom-call | tf_op jit(solution)/shard_map/jit(cholesky)/cholesky | solution.py:74
  543.0 10.2 %while.1 = (s32[]{:T(128)}, f32[512,512]{1,0:T(8,128)S(1)}, s32[4,2]{0,1:T(2,128)S(1)}, f32[4,128,128]{2,1,0:T(8,128)}, s32[]{:T(128)}) while((s32[]{:T(128)}, f32[512,512]{1,0:T(8,128)S(1)}, s32[4,2]{0,1:T(2,128)S(1)}, f32[4,128,128]{2,1,0:T(8,128)}, s32[]{:T(128)}) %tuple.94), condition=%wide.while_cond, body=%wide.while_body.sunk | while | flops 2 | bytes 132705 | solution.py:76
  553.2 40.1 %custom-call.33 = f32[4,128,128]{1,2,0:T(8,128)S(1)} custom-call(f32[4,128,128]{2,1,0:T(8,128)} %get-tuple-element.12), custom_call_target="InvertDiagBlocksLowerTriangular" | custom-call | tf_op jit(solution)/shard_map/triangular_solve | solution.py:76
  (178 shorter events, 122.8 us)
Async XLA Ops:
  6.5 5.8 copy-start
  6.5 446.4 %all-reduce.4.cloned.1.call-start = ((), (), s32[]{:S(2)}) async-start(), calls=%async_computation | async-start | bytes 2359296 | tf_op jit(solution)/shard_map/psum | solution.py:71
  6.5 28.2 %collective-permute-start.1 = (f32[4,16,32,128]{3,2,1,0:T(8,128)}, f32[4,16,32,128]{3,2,1,0:T(8,128)S(1)}, u32[]{:S(2)}, u32[]{:S(2)}) collective-permute-start(f32[4,16,32,128]{3,2,1,0:T(8,128)} %param.2), channel_id=1, source_target_pairs={{0,8},{8,16},{16,24},{24,0},{1,9},{9,17},{17,25},{25,1},{2,10},{10... | collective-permute-start | bytes 3145736 | tf_op jit(solution)/shard_map/ppermute | solution.py:20
  9.5 47.0 %collective-permute-start = (f32[4,16,32,128]{3,2,1,0:T(8,128)}, f32[4,16,32,128]{3,2,1,0:T(8,128)S(1)}, u32[]{:S(2)}, u32[]{:S(2)}) collective-permute-start(f32[4,16,32,128]{3,2,1,0:T(8,128)} %param.2), channel_id=1, source_target_pairs={{8,0},{16,8},{24,16},{0,24},{9,1},{17,9},{25,17},{1,25},{10,2},{18... | collective-permute-start | bytes 3145736 | tf_op jit(solution)/shard_map/ppermute | solution.py:21
  16.4 4.3 copy-start.12
  69.6 26.0 %collective-permute-start.2 = (f32[4,16,32,128]{3,2,1,0:T(8,128)S(1)}, f32[4,16,32,128]{3,2,1,0:T(8,128)S(1)}, u32[]{:S(2)}, u32[]{:S(2)}) collective-permute-start(f32[4,16,32,128]{3,2,1,0:T(8,128)S(1)} %get-tuple-element.23), channel_id=1, source_target_pairs={{8,0},{16,8},{24,16},{0,24},{9,1},{17,9},{25,17},{1,25},{10,2},{18... | collective-permute-start | bytes 3145736 | tf_op jit(solution)/shard_map/ppermute | solution.py:21
  71.0 45.2 %collective-permute-start.3 = (f32[4,16,32,128]{3,2,1,0:T(8,128)S(1)}, f32[4,16,32,128]{3,2,1,0:T(8,128)S(1)}, u32[]{:S(2)}, u32[]{:S(2)}) collective-permute-start(f32[4,16,32,128]{3,2,1,0:T(8,128)S(1)} %get-tuple-element.23), channel_id=1, source_target_pairs={{0,8},{8,16},{16,24},{24,0},{1,9},{9,17},{17,25},{25,1},{2,10},{10... | collective-permute-start | bytes 3145736 | tf_op jit(solution)/shard_map/ppermute | solution.py:20
  95.6 20.6 %copy-start.10 = (f32[4,16,32,128]{3,2,1,0:T(8,128)}, f32[4,16,32,128]{3,2,1,0:T(8,128)S(1)}, u32[]{:S(2)}) copy-start(f32[4,16,32,128]{3,2,1,0:T(8,128)S(1)} %collective-permute-done.2) | copy-start | bytes 3145732
  126.0 26.0 %collective-permute-start.4 = (f32[4,16,32,128]{3,2,1,0:T(8,128)S(1)}, f32[4,16,32,128]{3,2,1,0:T(8,128)S(1)}, u32[]{:S(2)}, u32[]{:S(2)}) collective-permute-start(f32[4,16,32,128]{3,2,1,0:T(8,128)S(1)} %multiply_subtract_fusion.2), channel_id=1, source_target_pairs={{8,0},{16,8},{24,16},{0,24},{9,1},{17,9},{25,17},{1,25},{10,2},{18... | collective-permute-start | bytes 3145736 | tf_op jit(solution)/shard_map/ppermute | solution.py:21
  128.3 44.2 %collective-permute-start.5 = (f32[4,16,32,128]{3,2,1,0:T(8,128)S(1)}, f32[4,16,32,128]{3,2,1,0:T(8,128)S(1)}, u32[]{:S(2)}, u32[]{:S(2)}) collective-permute-start(f32[4,16,32,128]{3,2,1,0:T(8,128)S(1)} %multiply_subtract_fusion.2), channel_id=1, source_target_pairs={{0,8},{8,16},{16,24},{24,0},{1,9},{9,17},{17,25},{25,1},{2,10},{10... | collective-permute-start | bytes 3145736 | tf_op jit(solution)/shard_map/ppermute | solution.py:20
  152.1 20.4 %copy-start.7 = (f32[4,16,32,128]{3,2,1,0:T(8,128)}, f32[4,16,32,128]{3,2,1,0:T(8,128)S(1)}, u32[]{:S(2)}) copy-start(f32[4,16,32,128]{3,2,1,0:T(8,128)S(1)} %collective-permute-done.4) | copy-start | bytes 3145732
  182.7 26.0 %collective-permute-start.6 = (f32[4,16,32,128]{3,2,1,0:T(8,128)S(1)}, f32[4,16,32,128]{3,2,1,0:T(8,128)S(1)}, u32[]{:S(2)}, u32[]{:S(2)}) collective-permute-start(f32[4,16,32,128]{3,2,1,0:T(8,128)S(1)} %multiply_subtract_fusion.1), channel_id=1, source_target_pairs={{8,0},{16,8},{24,16},{0,24},{9,1},{17,9},{25,17},{1,25},{10,2},{18... | collective-permute-start | bytes 3145736 | tf_op jit(solution)/shard_map/ppermute | solution.py:21
  184.1 44.0 %collective-permute-start.7 = (f32[4,16,32,128]{3,2,1,0:T(8,128)S(1)}, f32[4,16,32,128]{3,2,1,0:T(8,128)S(1)}, u32[]{:S(2)}, u32[]{:S(2)}) collective-permute-start(f32[4,16,32,128]{3,2,1,0:T(8,128)S(1)} %multiply_subtract_fusion.1), channel_id=1, source_target_pairs={{0,8},{8,16},{16,24},{24,0},{1,9},{9,17},{17,25},{25,1},{2,10},{10... | collective-permute-start | bytes 3145736 | tf_op jit(solution)/shard_map/ppermute | solution.py:20
  190.3 38.9 %copy-start.13 = (f32[4,16,32]{2,1,0:T(8,128)S(1)}, f32[4,16,32]{2,1,0:T(8,128)}, u32[]{:S(2)}) copy-start(f32[4,16,32]{2,1,0:T(8,128)} %param.3) | copy-start | bytes 24580
  208.7 19.4 %copy-start.6 = (f32[4,16,32,128]{3,2,1,0:T(8,128)}, f32[4,16,32,128]{3,2,1,0:T(8,128)S(1)}, u32[]{:S(2)}) copy-start(f32[4,16,32,128]{3,2,1,0:T(8,128)S(1)} %collective-permute-done.6) | copy-start | bytes 3145732
  237.6 6.8 %collective-permute-start.8 = (f32[2048,64]{0,1:T(8,128)S(1)}, f32[2048,64]{0,1:T(8,128)}, u32[]{:S(2)}, u32[]{:S(2)}) collective-permute-start(f32[2048,64]{0,1:T(8,128)S(1)} %copy.11), channel_id=1, source_target_pairs={{0,7},{1,0},{2,1},{3,2},{4,3},{5,4},{6,5},{7,6},{8,15},{9,8},{10,9... | collective-permute-start | bytes 1572872 | tf_op jit(solution)/shard_map/ppermute | solution.py:65
  246.0 26.2 %collective-permute-start.9 = (f32[2048,128]{1,0:T(8,128)S(1)}, f32[2048,128]{1,0:T(8,128)S(1)}, u32[]{:S(2)}, u32[]{:S(2)}) collective-permute-start(f32[2048,128]{1,0:T(8,128)S(1)} %pad_maximum_fusion.7), channel_id=1, source_target_pairs={{0,6},{1,7},{2,0},{3,1},{4,2},{5,3},{6,4},{7,5},{8,14},{9,15},{10,... | collective-permute-start | bytes 3145736 | tf_op jit(solution)/shard_map/ppermute | solution.py:65
  272.2 2.0 copy-start.1
  274.1 94.2 %collective-permute-start.10 = (f32[2048,256]{1,0:T(8,128)}, f32[2048,256]{1,0:T(8,128)}, u32[]{:S(2)}, u32[]{:S(2)}) collective-permute-start(f32[2048,256]{1,0:T(8,128)} %pad_maximum_fusion), channel_id=1, source_target_pairs={{0,4},{1,5},{2,6},{3,7},{4,0},{5,1},{6,2},{7,3},{8,12},{9,13},{10,... | collective-permute-start | bytes 6291464 | tf_op jit(solution)/shard_map/ppermute | solution.py:65
  453.0 1.8 copy-start.2
  512.1 81.5 %copy-start.4 = (f32[512,512]{1,0:T(8,128)S(1)}, f32[512,512]{1,0:T(8,128)}, u32[]{:S(2)}) copy-start(f32[512,512]{1,0:T(8,128)} %fusion.136) | copy-start | bytes 3145732
  594.0 11.2 %slice-start = ((s8[8388608]{0:T(1024)(128)(4,1)}), s8[4194304]{0:T(1024)(128)(4,1)S(1)}, s32[]{:S(2)}) async-start(s8[8388608]{0:T(1024)(128)(4,1)} %bitcast.52), calls=%async_computation.1 | async-start | bytes 8388608
  596.5 8.8 %slice-start.1 = ((s8[8388608]{0:T(1024)(128)(4,1)}), s8[4194304]{0:T(1024)(128)(4,1)S(1)}, s32[]{:S(2)}) async-start(s8[8388608]{0:T(1024)(128)(4,1)} %bitcast.52), calls=%async_computation.2 | async-start | bytes 8388608
  598.4 6.8 %copy-start.5 = (f32[2048,64]{0,1:T(8,128)S(1)}, f32[2048,64]{0,1:T(8,128)}, u32[]{:S(2)}) copy-start(f32[2048,64]{0,1:T(8,128)} %copy.21) | copy-start | bytes 1572868
  (5 other events, 5.4 us)
Sparse Core Ops, SparseCore 0:
  398.3 54.6 all-reduce.3
